TPU v7x, 32 devices: a whole 2x2x4 slice. The times are simulated.
32 devices in a mesh: groups: 2 (over x), grid: 16 (over z, y, core).
Axes of the slice: x: 2, y: 2, z: 4, core: 2. Of those that a mesh axis runs over, the one named last changes fastest.
Arguments:
- spectra: bfloat16 [512, 4096], P('groups', 'grid'), parts along dimension 0, may hold values from -6 to 6
- response: bfloat16 [4096, 2048], P('grid'), may hold values from -0.09375 to 0.09375
- observed: float32 [1024, 32], P(('groups', 'grid')), parts along dimension 0, may hold values from -6 to 6
- inv_var: float32 [1024, 32], P(('groups', 'grid')), parts along dimension 0, may hold values from 0.5 to 4
- band_mask: int32 [1024, 32], P(('groups', 'grid')), parts along dimension 0, may hold values from 0 to 1
- det_counts: int32 [1024], P(('groups', 'grid')), parts along dimension 0, may hold values from 4 to 32
- anchor_bins: int32 [1024], P(('groups', 'grid')), parts along dimension 0, may hold values from -1 to 63, as said below
- init_weights: float32 [32768], P(('groups', 'grid')), parts along dimension 0, may hold values from 0.1 to 10
Outputs:
- weights: float32 [32768], P(('groups', 'grid')), parts along dimension 0
- posterior: float32 [64, 1024], P(None, ('groups', 'grid')), parts along dimension 1
There are 2 independent parts, one for each index of `groups`. A program takes and returns all parts, laid end to end along the dimension named above; an argument that names none is the same for every part. Nothing has to cross between parts.
Inputs may be any that keep to these rules, and one draw needn't show every extreme that they name: `anchor_bins`: a bin index of 0 to 63 for a galaxy with a spectroscopic redshift, -1 for the others.
All inputs are finite; a program needn't handle non-finite values.
Results may differ from a plain program's by a relative error of at most 0.006.
The roundings to bfloat16 on the way count: a program that leaves them out, or rounds other values in their place, can miss the bound.
Values may be sent and summed in bfloat16 or wider, within the bound.
A program may use at most 64 MiB of HBM per device.

v0:
```python
import jax
import jax.numpy as jnp
from jax import lax
from jax.sharding import PartitionSpec as P

REDSHIFTS = 64
BANDS = 32
STEPS = 2


excluded_score = -1e30


def combined_all(array, axis, combine):
    everything = jax.tree.map(lambda part: lax.all_gather(part, axis), array)
    first = jax.tree.map(lambda part: part[0], everything)

    def turn(k, so_far):
        return combine(so_far, jax.tree.map(lambda part: part[k], everything))

    return lax.fori_loop(1, lax.axis_size(axis), turn, first)


def model_columns(fluxes):
    shaped = fluxes.reshape(-1, REDSHIFTS, BANDS)
    joined = jnp.concatenate((-2.0 * shaped, shaped * shaped), axis=2)
    return joined.astype(jnp.bfloat16).reshape(-1, 2 * BANDS)


def galaxy_coeffs(observed, inv_var, band_mask, det_counts):
    masked_var = inv_var * band_mask.astype(jnp.float32)
    temper = 4.0 / (det_counts.astype(jnp.float32) + 8.0)
    joined = jnp.concatenate((masked_var * observed, masked_var), axis=1)
    return (temper[:, None] * joined).astype(jnp.bfloat16)


def block_scores(row_block, bin_block, model_cols):
    scores = -jnp.dot(row_block, model_cols.T, preferred_element_type=jnp.float32)
    column_bin = jnp.arange(model_cols.shape[0], dtype=jnp.int32) % REDSHIFTS
    allowed = (bin_block[:, None] < 0) | (bin_block[:, None] == column_bin[None, :])
    return jnp.where(allowed, scores, excluded_score)


def combine_norms(first, second):
    peak = jnp.maximum(first[0], second[0])
    total = first[1] * jnp.exp(first[0] - peak) + second[1] * jnp.exp(second[0] - peak)
    return (peak, total)


def on_device(
    spectra, response, observed, inv_var, band_mask, det_counts, anchor_bins, init_weights
):
    fluxes = lax.psum_scatter(
        jnp.dot(spectra, response, preferred_element_type=jnp.float32),
        "grid",
        scatter_dimension=0,
        tiled=True,
    )
    model_cols = model_columns(fluxes)
    coeffs = galaxy_coeffs(observed, inv_var, band_mask, det_counts)
    all_rows = lax.all_gather(coeffs, "grid", axis=0, tiled=True)
    all_bins = lax.all_gather(anchor_bins, "grid", axis=0, tiled=True)
    galaxies = all_rows.shape[0]
    block = min(512, galaxies)
    count_blocks = galaxies // block
    row_blocks = all_rows.reshape(count_blocks, block, 2 * BANDS)
    bin_blocks = all_bins.reshape(count_blocks, block)
    weights = init_weights
    posterior = None
    for em_step in range(STEPS):

        def local_pair(carry, pair, weights=weights):
            scores = block_scores(pair[0], pair[1], model_cols)
            peak = jnp.max(scores, axis=1)
            total = jnp.sum(weights[None, :] * jnp.exp(scores - peak[:, None]), axis=1)
            return (carry, (peak, total))

        unused, (peaks, totals) = lax.scan(
            local_pair, jnp.zeros((), jnp.float32), (row_blocks, bin_blocks)
        )
        peaks, totals = combined_all((peaks.reshape(-1), totals.reshape(-1)), "grid", combine_norms)
        log_norm = peaks + jnp.log(totals)

        def responsibilities(carry, triple, weights=weights):
            scores = block_scores(triple[0], triple[1], model_cols)
            shares = weights[None, :] * jnp.exp(scores - triple[2][:, None])
            return (
                carry + jnp.sum(shares, axis=0),
                jnp.sum(shares.reshape(block, -1, REDSHIFTS), axis=1),
            )

        mass, posterior = lax.scan(
            responsibilities,
            jnp.zeros((model_cols.shape[0],), jnp.float32),
            (row_blocks, bin_blocks, log_norm.reshape(count_blocks, block)),
        )
        weights = mass / galaxies
    posterior_terms = posterior.reshape(galaxies, REDSHIFTS).T
    posterior_own = lax.psum_scatter(posterior_terms, "grid", scatter_dimension=1, tiled=True)
    return (weights, posterior_own)


def solution(mesh):
    return jax.shard_map(
        on_device,
        mesh=mesh,
        in_specs=(
            P("groups", "grid"),
            P("grid", None),
            P(("groups", "grid"), None),
            P(("groups", "grid"), None),
            P(("groups", "grid"), None),
            P(("groups", "grid")),
            P(("groups", "grid")),
            P(("groups", "grid")),
        ),
        out_specs=(P(("groups", "grid")), P(None, ("groups", "grid"))),
        check_vma=False,
    )
```

profile of v0, /device:TPU:0, one launch (start us, length us, event | category | flops | bytes accessed | tf_op | source)
XLA Modules:
  0.0 203.2 jit_solution(7234537589837447197)
XLA Ops:
  7.2 0.0 copy-start
  7.2 0.0 copy-start.7
  7.2 0.0 copy-start.5
  7.2 0.0 copy-start.6
  7.2 0.0 copy-start.4
  7.2 0.0 copy-start.3
  7.2 0.0 copy-start.2
  7.2 0.0 reduce-scatter.5.cloned.1.call-start
  7.3 1.1 copy-done
  8.4 2.7 %fusion.11 = f32[256,2048]{1,0:T(8,128)} fusion(bf16[256,256]{1,0:T(8,128)(2,1)} %param.12, bf16[256,2048]{1,0:T(8,128)(2,1)S(1)} %copy-done), kind=kOutput, calls=%fused_computation.38 | convolution fusion | flops 268435456 | bytes 3276800 | tf_op jit(solution)/shard_map/dot_general | solution.py:54
  11.1 0.0 reduce-scatter.5.cloned.1.call-update
  11.1 0.0 reduce-scatter.7.cloned.1.call-start
  11.2 0.0 copy-done.7
  11.2 0.6 dynamic-slice.4
  12.4 0.0 copy-done.5
  12.4 0.2 dynamic-update-slice
  12.7 13.7 %all-reduce = s32[512]{0:T(512)S(1)} all-reduce(s32[512]{0:T(512)S(1)} %dynamic-update-slice), channel_id=1, replica_groups=mesh['groups'=2,'grid'=16] {'grid'}, use_global_device_ids=true, to_apply=%add | all-reduce | flops 512 | bytes 4096
  26.4 0.0 copy-done.6
  26.4 0.0 copy-done.4
  26.4 0.0 copy-done.3
  26.4 0.0 copy-done.2
  26.5 0.1 fusion.3
  26.5 18.3 %all_gather.17 = bf16[512,64]{1,0:T(8,128)(2,1)S(1)} all-gather(bf16[32,64]{1,0:T(8,128)(2,1)S(1)} %fusion.3), channel_id=1, replica_groups=mesh['groups'=2,'grid'=16] {'grid'}, dimensions={0}, use_global_device_ids=true | all-gather | bytes 69632 | tf_op jit(solution)/shard_map/all_gather | solution.py:61
  44.8 0.5 broadcast_compare_fusion
  45.3 30.8 %reduce-scatter.5.cloned.1.call-done = f32[16,2048]{1,0:T(8,128)} async-done(((f32[256,2048]{1,0:T(8,128)}), f32[16,2048]{1,0:T(8,128)}) %reduce-scatter.5.cloned.1.call-update) | async-done | bytes 131088 | tf_op jit(solution)/shard_map/reduce_scatter | solution.py:53
  76.1 0.9 multiply_convert_fusion.1
  77.0 0.0 copy-start.1
  77.0 0.2 mul.122
  77.2 0.9 mul.124
  78.1 1.7 fusion.10
  79.9 0.0 copy-done.1
  79.9 0.5 multiply_reduce_fusion.2
  80.4 19.5 %all-gather.4 = f32[16,1,512]{2,1,0:T(1,128)S(1)} all-gather(f32[1,1,512]{2,1,0:T(1,128)S(1)} %bitcast.51), channel_id=3, replica_groups=mesh['groups'=2,'grid'=16] {'grid'}, dimensions={0}, use_global_device_ids=true | all-gather | bytes 34816 | tf_op jit(solution)/shard_map/all_gather | solution.py:15
  99.9 17.5 %all-gather.3 = f32[16,1,512]{2,1,0:T(1,128)S(1)} all-gather(f32[1,1,512]{2,1,0:T(1,128)S(1)} %bitcast.49), channel_id=2, replica_groups=mesh['groups'=2,'grid'=16] {'grid'}, dimensions={0}, use_global_device_ids=true | all-gather | bytes 34816 | tf_op jit(solution)/shard_map/all_gather | solution.py:15
  117.4 0.9 while.22
  118.2 0.4 multiply_reduce_fusion.1
  118.7 0.5 multiply_reduce_fusion
  119.2 18.9 %all-gather.5 = f32[16,1,512]{2,1,0:T(1,128)S(1)} all-gather(f32[1,1,512]{2,1,0:T(1,128)S(1)} %bitcast.50), channel_id=4, replica_groups=mesh['groups'=2,'grid'=16] {'grid'}, dimensions={0}, use_global_device_ids=true | all-gather | bytes 34816 | tf_op jit(solution)/shard_map/all_gather | solution.py:15
  138.1 0.9 while.23
  139.0 1.8 fusion.8
  140.7 1.9 copy.13
  142.6 0.2 reduce_sum.54
  142.8 0.8 copy.15
  143.6 0.0 reduce-scatter.7.cloned.1.call-update
  143.7 0.6 broadcast_multiply_fusion
  144.3 52.1 %reduce-scatter.7.cloned.1.call-done = f32[32,64]{1,0:T(8,128)} async-done(((f32[512,64]{1,0:T(8,128)}), f32[32,64]{1,0:T(8,128)}) %reduce-scatter.7.cloned.1.call-update) | async-done | bytes 8208
  (74 shorter events, 1.0 us)
Async XLA Ops:
  7.2 1.2 copy-start
  7.2 4.0 %copy-start.7 = (u32[32]{0:T(128)S(1)}, u32[32]{0:T(128)}, u32[]{:S(2)}) copy-start(u32[32]{0:T(128)} %constant.182) | copy-start | bytes 388
  7.2 5.2 %copy-start.5 = (s32[32]{0:T(128)S(1)}, s32[32]{0:T(128)}, u32[]{:S(2)}) copy-start(s32[32]{0:T(128)} %param.18) | copy-start | bytes 388
  7.2 19.2 %copy-start.6 = (s32[32]{0:T(128)S(1)}, s32[32]{0:T(128)}, u32[]{:S(2)}) copy-start(s32[32]{0:T(128)} %param.17) | copy-start | bytes 388
  7.2 19.2 %copy-start.4 = (s32[32,32]{1,0:T(8,128)S(1)}, s32[32,32]{1,0:T(8,128)}, u32[]{:S(2)}) copy-start(s32[32,32]{1,0:T(8,128)} %param.16) | copy-start | bytes 12292
  7.2 19.2 %copy-start.3 = (f32[32,32]{1,0:T(8,128)S(1)}, f32[32,32]{1,0:T(8,128)}, u32[]{:S(2)}) copy-start(f32[32,32]{1,0:T(8,128)} %param.15) | copy-start | bytes 12292
  7.2 19.2 %copy-start.2 = (f32[32,32]{1,0:T(8,128)S(1)}, f32[32,32]{1,0:T(8,128)}, u32[]{:S(2)}) copy-start(f32[32,32]{1,0:T(8,128)} %param.14) | copy-start | bytes 12292
  7.2 68.9 %reduce-scatter.5.cloned.1.call-start = ((), (), s32[]{:S(2)}) async-start(), calls=%async_computation.2 | async-start | bytes 2228224 | tf_op jit(solution)/shard_map/reduce_scatter | solution.py:53
  11.1 185.2 %reduce-scatter.7.cloned.1.call-start = ((), (), s32[]{:S(2)}) async-start(), calls=%async_computation.3 | async-start | bytes 278528
  77.0 2.8 %copy-start.1 = (f32[1024]{0:T(1024)S(1)}, f32[1024]{0:T(1024)}, u32[]{:S(2)}) copy-start(f32[1024]{0:T(1024)} %param.19) | copy-start | bytes 12292
Sparse Core Ops, SparseCore 0:
  11.8 64.2 reduce-scatter.4
  143.8 52.5 reduce-scatter.6
where the time goes:
time: 203 us
  blocking collectives  87.8 us (43%)
  waiting for transfers between devices  82.9 us (41%)
  between operations  14.9 us (7%)
  local copies, waits for them, and re-layouts  6.16 us (3%)
  other arithmetic  6.16 us (3%)
  matrix products  4.44 us (2%)
    all_gather x3, blocking collectives, combined_all(): everything = jax.tree.map(lambda part: lax.all_gather(part, axis), array)  55.8 us
    unnamed x3, waiting for transfers between devices  52.1 us
    reduce_scatter x1, waiting for transfers between devices, on_device(): lax.psum_scatter(jnp.dot(spectra, response, preferred_element_type=jnp.fl...  30.8 us
    all_gather x1, blocking collectives, on_device(): all_rows = lax.all_gather(coeffs, 'grid', axis=0, tiled=True)  18.3 us
    unnamed x1, blocking collectives  13.7 us
  transfers between devices with their start and end apart: 2, of which 2 were waited for; matrix products, arithmetic and copies ran while one was open for 1% of the time, Pallas kernels for 0%

commit v1 on v0

v1 whole, which is shorter than its diff:
```python
import functools

import jax
import jax.numpy as jnp
from jax import lax
from jax.experimental import pallas as pl
from jax.experimental.pallas import tpu as pltpu
from jax.sharding import PartitionSpec as P

REDSHIFTS = 64
BANDS = 32
STEPS = 2
LANES = 128
QUARTERS = LANES // BANDS
GROUPS_Z = REDSHIFTS // QUARTERS
CHUNKS = 4
MESH = pl.DeviceIdType.MESH
EXCLUDED = -1e30
HIGHEST = lax.Precision.HIGHEST


def iota(shape, dim):
    return lax.broadcasted_iota(jnp.int32, shape, dim)


def over_quarters(x, op):
    x = op(x, pltpu.roll(x, 64, 1))
    return op(x, pltpu.roll(x, 32, 1))


def body(
    n,
    galaxies,
    spectra_ref,
    response_ref,
    rows_ref,
    w_ref,
    outw_ref,
    outp_ref,
    part,
    got_a,
    got_b,
    got_c,
    all_rows,
    rt,
    penalty,
    cols,
    e_ref,
    wts,
    norms,
    x_ref,
    tots,
    post,
    got_post,
    a_send,
    a_recv,
    b_send,
    b_recv,
    c_send,
    c_recv,
    r_send,
    r_recv,
    n_send,
    n_recv,
    t_send,
    t_recv,
    p_send,
    p_recv,
):
    group = lax.axis_index("groups")
    me = lax.axis_index("grid")
    core = lax.rem(me, 2)
    yy = lax.rem(me // 2, 2)
    zz = me // 4
    nz = n // 4
    width = part.shape[-1]
    models = part.shape[-2]

    barrier = pltpu.get_barrier_semaphore()

    @pl.loop(1, n)
    def _(s):
        pl.semaphore_signal(
            barrier, inc=1, device_id=(group, lax.rem(me + s, n)), device_id_type=MESH
        )

    def flux_part(k):
        block = jnp.dot(
            spectra_ref[...],
            response_ref[:, k * width : (k + 1) * width],
            preferred_element_type=jnp.float32,
        )
        part[k] = block.reshape(nz, 2, 2, models, width)

    flux_part(0)
    pl.semaphore_wait(barrier, n - 1)

    def copy(src, dst, send, recv, target):
        return pltpu.make_async_remote_copy(
            src_ref=src,
            dst_ref=dst,
            send_sem=send,
            recv_sem=recv,
            device_id=(group, target),
            device_id_type=MESH,
        )

    def copy_a(k):
        return copy(
            part.at[k, :, :, 1 - core], got_a.at[k], a_send.at[k], a_recv.at[k], me + 1 - 2 * core
        )

    def copy_b(k):
        return copy(
            got_a.at[k, :, 1 - yy], got_b.at[k], b_send.at[k], b_recv.at[k], me + 2 - 4 * yy
        )

    def copy_c(k, s):
        to = lax.rem(zz + s, nz)
        return copy(
            got_b.at[k, to],
            got_c.at[k, s],
            c_send.at[k, s],
            c_recv.at[k, s],
            lax.rem(me + 4 * s, n),
        )

    copy_a(0).start()
    for k in range(1, CHUNKS):
        flux_part(k)
        copy_a(k).start()

    def spread(src, dst, send, recv, s):
        return copy(src, dst, send.at[s], recv.at[s], lax.rem(me + s, n))

    def rows_copy(s):
        return spread(rows_ref, all_rows.at[me], r_send, r_recv, s)

    all_rows[me] = rows_ref[...]

    for k in range(CHUNKS):
        copy_a(k).wait()
        for z in range(nz):
            for y in range(2):
                got_a[k, z, y] = got_a[k, z, y] + part[k, z, y, core]
        copy_b(k).start()

    @pl.loop(1, n)
    def _(s):
        rows_copy(s).start()

    for k in range(CHUNKS):
        copy_b(k).wait()
        for z in range(nz):
            got_b[k, z] = got_b[k, z] + got_a[k, z, yy]
        for s in range(1, nz):
            copy_c(k, s).start()

    eight = w_ref.shape[0]
    pick = (iota((models, eight), 0) // 2 == iota((models, eight), 1)).astype(jnp.float32)
    both = jnp.dot(pick, w_ref[...], precision=HIGHEST, preferred_element_type=jnp.float32)
    own = iota((models, LANES), 1) // REDSHIFTS == lax.rem(iota((models, LANES), 0), 2)
    both = jnp.where(own, both, 0.0)
    for j in range(GROUPS_Z):
        spot = lax.rem(iota((LANES, LANES), 0), REDSHIFTS) == 4 * j + iota((LANES, LANES), 1) // BANDS
        wts[j * models : (j + 1) * models, :] = jnp.dot(
            both, spot.astype(jnp.float32), precision=HIGHEST, preferred_element_type=jnp.float32
        )

    @pl.loop(1, n)
    def _(s):
        rows_copy(s).wait()

    lane = lax.rem(iota((LANES, 2 * LANES), 1), BANDS) + BANDS * (iota((LANES, 2 * LANES), 1) // LANES)
    tiles = (iota((LANES, 2 * LANES), 0) == lane).astype(jnp.bfloat16)
    keep = lax.rem(iota((LANES, 2 * LANES), 1), LANES) // BANDS == iota((LANES, 2 * LANES), 0) // BANDS
    anchor_row = (iota((GROUPS_Z, LANES), 1) == 2 * BANDS).astype(jnp.bfloat16)
    zbin = (QUARTERS * iota((GROUPS_Z, LANES), 0) + iota((GROUPS_Z, LANES), 1) // BANDS).astype(
        jnp.float32
    )

    @pl.loop(0, n)
    def _(d):
        x = all_rows[d]
        x = jnp.concatenate([x] * QUARTERS, axis=0)
        y = jnp.dot(x, tiles, preferred_element_type=jnp.float32)
        rt[d] = jnp.where(keep, y, 0.0).astype(jnp.bfloat16)
        anchors = lax.dot_general(
            anchor_row, x, (((1,), (1,)), ((), ())), preferred_element_type=jnp.float32
        )
        penalty[d] = jnp.where((anchors < 0) | (anchors == zbin), 0.0, EXCLUDED)

    per = width // LANES
    for k in range(CHUNKS):
        for s in range(1, nz):
            copy_c(k, s).wait()
        flux = got_b[k, zz]
        for s in range(1, nz):
            flux = flux + got_c[k, s]
        for i in range(per):
            j = k * per + i
            f = flux[:, i * LANES : (i + 1) * LANES]
            cols[j * models : (j + 1) * models, 0:LANES] = (2.0 * f).astype(jnp.bfloat16)
            cols[j * models : (j + 1) * models, LANES : 2 * LANES] = (-(f * f)).astype(jnp.bfloat16)

    rows_all = GROUPS_Z * models

    @pl.loop(0, n)
    def _(d):
        scores = lax.dot_general(
            cols[...], rt[d], (((1,), (1,)), ((), ())), preferred_element_type=jnp.float32
        )
        scores = scores.reshape(GROUPS_Z, models, LANES) + penalty[d][:, None, :]
        scores = scores.reshape(rows_all, LANES)
        peak = over_quarters(jnp.max(scores, axis=0, keepdims=True), jnp.maximum)
        e = jnp.exp(scores - peak)
        e_ref[d] = e
        total = over_quarters(jnp.sum(e * wts[...], axis=0, keepdims=True), jnp.add)
        norms[me, 0, pl.ds(d, 1), :] = peak
        norms[me, 1, pl.ds(d, 1), :] = total

    def norms_copy(s):
        return spread(norms.at[me], norms.at[me], n_send, n_recv, s)

    @pl.loop(1, n)
    def _(s):
        norms_copy(s).start()

    def norms_wait(s):
        src = lax.rem(me + n - s, n)
        return copy(norms.at[src], norms.at[src], n_send.at[s], n_recv.at[s], lax.rem(me + s, n))

    @pl.loop(1, n)
    def _(s):
        norms_wait(s).wait()

    top = norms[0, 0]
    for d in range(1, n):
        top = jnp.maximum(top, norms[d, 0])
    total = jnp.zeros_like(top)
    for d in range(n):
        total = total + norms[d, 1] * jnp.exp(norms[d, 0] - top)
    x_ref[0] = jnp.exp(norms[me, 0] - top)
    x_ref[1] = x_ref[0] / total

    same = (iota((LANES, LANES), 0) // BANDS == iota((LANES, LANES), 1) // BANDS).astype(jnp.float32)

    def new_weights():
        def add(d, acc):
            return acc + e_ref[d] * x_ref[1, pl.ds(d, 1), :]

        mass = lax.fori_loop(0, n, add, jnp.zeros((rows_all, LANES), jnp.float32))
        mass = jnp.dot(mass, same, precision=HIGHEST, preferred_element_type=jnp.float32)
        wts[...] = wts[...] * mass * (1.0 / galaxies)

    new_weights()

    @pl.loop(0, n)
    def _(d):
        v = (e_ref[d] * wts[...]).reshape(GROUPS_Z, models, LANES)
        u = jnp.sum(v, axis=1) * x_ref[0, pl.ds(d, 1), :]
        post[d] = u
        tots[me, pl.ds(d, 1), :] = over_quarters(jnp.sum(u, axis=0, keepdims=True), jnp.add)

    def tots_copy(s):
        return spread(tots.at[me], tots.at[me], t_send, t_recv, s)

    def post_copy(s):
        to = lax.rem(me + s, n)
        return copy(post.at[to], got_post.at[s], p_send.at[s], p_recv.at[s], to)

    @pl.loop(1, n)
    def _(s):
        tots_copy(s).start()

    @pl.loop(1, n)
    def _(s):
        post_copy(s).start()

    def tots_wait(s):
        src = lax.rem(me + n - s, n)
        return copy(tots.at[src], tots.at[src], t_send.at[s], t_recv.at[s], lax.rem(me + s, n))

    @pl.loop(1, n)
    def _(s):
        tots_wait(s).wait()

    total = tots[0]
    for d in range(1, n):
        total = total + tots[d]
    x_ref[1] = x_ref[0] / total
    new_weights()

    out = jnp.zeros((models, REDSHIFTS), jnp.float32)
    for j in range(GROUPS_Z):
        spot = iota((LANES, REDSHIFTS), 0) == BANDS * (iota((LANES, REDSHIFTS), 1) - 4 * j)
        out = out + jnp.dot(
            wts[j * models : (j + 1) * models, :],
            spot.astype(jnp.float32),
            precision=HIGHEST,
            preferred_element_type=jnp.float32,
        )
    outw_ref[...] = out

    @pl.loop(1, n)
    def _(s):
        post_copy(s).wait()

    mine = post[me]
    for s in range(1, n):
        mine = mine + got_post[s]
    whole = over_quarters(jnp.sum(mine, axis=0, keepdims=True), jnp.add)
    outp_ref[...] = mine / whole


def galaxy_rows(observed, inv_var, band_mask, det_counts, anchor_bins):
    masked_var = inv_var * band_mask.astype(jnp.float32)
    temper = 4.0 / (det_counts.astype(jnp.float32) + 8.0)
    joined = jnp.concatenate((masked_var * observed, masked_var), axis=1)
    joined = temper[:, None] * joined
    own = observed.shape[0]
    last = jnp.zeros((own, LANES - 2 * BANDS - 1), jnp.float32)
    anchors = anchor_bins.astype(jnp.float32)[:, None]
    return jnp.concatenate((joined, anchors, last), axis=1).astype(jnp.bfloat16)


def on_device(
    n, spectra, response, observed, inv_var, band_mask, det_counts, anchor_bins, init_weights
):
    rows = galaxy_rows(observed, inv_var, band_mask, det_counts, anchor_bins)
    own = observed.shape[0]
    models = spectra.shape[0] // n
    nz = n // 4
    width = response.shape[1] // CHUNKS
    f32, bf16 = jnp.float32, jnp.bfloat16
    dma = pltpu.SemaphoreType.DMA
    lanes_g = QUARTERS * own
    rows_all = GROUPS_Z * models
    weights, posterior = pl.pallas_call(
        functools.partial(body, n, own * n),
        out_shape=(
            jax.ShapeDtypeStruct((models, REDSHIFTS), f32),
            jax.ShapeDtypeStruct((GROUPS_Z, lanes_g), f32),
        ),
        in_specs=[pl.BlockSpec(memory_space=pltpu.VMEM)] * 4,
        out_specs=[pl.BlockSpec(memory_space=pltpu.VMEM)] * 2,
        scratch_shapes=[
            pltpu.VMEM((CHUNKS, nz, 2, 2, models, width), f32),
            pltpu.VMEM((CHUNKS, nz, 2, models, width), f32),
            pltpu.VMEM((CHUNKS, nz, models, width), f32),
            pltpu.VMEM((CHUNKS, nz, models, width), f32),
            pltpu.VMEM((n, own, LANES), bf16),
            pltpu.VMEM((n, LANES, 2 * LANES), bf16),
            pltpu.VMEM((n, GROUPS_Z, LANES), f32),
            pltpu.VMEM((rows_all, 2 * LANES), bf16),
            pltpu.VMEM((n, rows_all, LANES), f32),
            pltpu.VMEM((rows_all, LANES), f32),
            pltpu.VMEM((n, 2, n, LANES), f32),
            pltpu.VMEM((2, n, LANES), f32),
            pltpu.VMEM((n, n, LANES), f32),
            pltpu.VMEM((n, GROUPS_Z, LANES), f32),
            pltpu.VMEM((n, GROUPS_Z, LANES), f32),
            dma((CHUNKS,)),
            dma((CHUNKS,)),
            dma((CHUNKS,)),
            dma((CHUNKS,)),
            dma((CHUNKS, nz)),
            dma((CHUNKS, nz)),
        ]
        + [dma((n,))] * 8,
        compiler_params=pltpu.CompilerParams(
            collective_id=0, has_side_effects=True, vmem_limit_bytes=56 * 2**20
        ),
    )(spectra, response, rows, init_weights.reshape(-1, LANES))
    return weights.reshape(-1), posterior.reshape(REDSHIFTS, own)


def solution(mesh):
    return jax.shard_map(
        functools.partial(on_device, mesh.shape["grid"]),
        mesh=mesh,
        in_specs=(
            P("groups", "grid"),
            P("grid", None),
            P(("groups", "grid"), None),
            P(("groups", "grid"), None),
            P(("groups", "grid"), None),
            P(("groups", "grid")),
            P(("groups", "grid")),
            P(("groups", "grid")),
        ),
        out_specs=(P(("groups", "grid")), P(None, ("groups", "grid"))),
        check_vma=False,
    )
```

time: 203 us -> 60.6 us (0.30)
  blocking collectives: 87.8 us -> 0 us
  waiting for transfers between devices: 82.9 us -> 0 us
  Pallas kernels: 0 us -> 54.5 us
  between operations: 14.9 us -> 0.67 us
  matrix products: 4.44 us -> 0 us
  other arithmetic: 6.16 us -> 2.17 us
  local copies, waits for them, and re-layouts: 6.16 us -> 2.95 us
    all_gather x4 -> x0, blocking collectives: 74.1 us -> none  [the longest x3 55.8 us: combined_all(): everything = jax.tree.map(lambda part: lax.all_gather(part, axis), array)]
    pallas_call x0 -> x1, Pallas kernels: none -> 54.5 us  [on_device(): pl.pallas_call(functools.partial(body, n, own * n), out_shape=(jax.ShapeD...]
    unnamed x3 -> x0, waiting for transfers between devices: 52.1 us -> none
    reduce_scatter x1 -> x0, waiting for transfers between devices: 30.8 us -> none  [on_device(): lax.psum_scatter(jnp.dot(spectra, response, preferred_element_type=jnp.fl...]
    unnamed x1 -> x0, blocking collectives: 13.7 us -> none
    dot_general x2 -> x0, matrix products: 4.44 us -> none  [the longest x1 2.7 us: on_device(): jnp.dot(spectra, response, preferred_element_type=jnp.float32)]
    reduce_sum x5 -> x0, other arithmetic: 3.4 us -> none  [the longest x2 2.19 us: responsibilities(): jnp.sum(shares, axis=0)]
    mul x3 -> x0, local copies, waits for them, and re-layouts: 2.99 us -> none  [the longest x1 1.92 us: responsibilities(): shares = weights[None, :] * jnp.exp(scores - triple[2][:, None])]
  transfers between devices with their start and end apart: 2 -> 0, of which waited for: 2 -> 0; matrix products, arithmetic and copies ran while one was open for 1% -> 0% of each run, Pallas kernels for 0% -> 0%
where the time goes in v1:
time: 60.6 us; the launch traced here: 60.3 us
  Pallas kernels  54.5 us (90%)
  local copies, waits for them, and re-layouts  2.95 us (5%)
  other arithmetic  2.17 us (4%)
  between operations  0.67 us (1%)
    pallas_call x1, Pallas kernels, on_device(): pl.pallas_call(functools.partial(body, n, own * n), out_shape=(jax.ShapeD...  54.5 us
    reshape x2, local copies, waits for them, and re-layouts, on_device(): return (weights.reshape(-1), posterior.reshape(REDSHIFTS, own))  1.43 us
    unnamed x7, local copies, waits for them, and re-layouts  1.33 us

profile of v1, /device:TPU:0, one launch (start us, length us, event | category | flops | bytes accessed | tf_op | source)
XLA Modules:
  0.0 60.3 jit_solution(13181889180087579737)
XLA Ops:
  0.6 0.0 copy-start.2
  0.6 0.0 copy-start
  0.6 0.6 %copy-done.2 = s32[32]{0:T(128)S(1)} copy-done((s32[32]{0:T(128)S(1)}, s32[32]{0:T(128)}, u32[]{:S(2)}) %copy-start.2) | copy-done | bytes 152
  1.3 0.7 %convert_bitcast_fusion = bf16[32,1]{0,1:T(2,128)(2,1)S(1)} fusion(s32[32]{0:T(128)} %param.14), kind=kLoop, calls=%fused_computation.4 | loop fusion | flops 64 | bytes 192 | tf_op jit(solution)/shard_map/broadcast_in_dim | solution.py:323
  2.0 0.1 pad.2.clone
  2.0 0.1 copy.12
  2.1 0.0 copy-done
  2.1 0.7 %fusion.1 = (f32[32,32]{1,0:T(8,128)S(1)}, f32[32,32]{1,0:T(8,128)S(1)}) fusion(f32[32,32]{1,0:T(8,128)S(1)} %copy-done, f32[32,32]{1,0:T(8,128)} %param.11, s32[32,32]{1,0:T(8,128)} %param.12), kind=kLoop, calls=%fused_computation.6 | loop fusion | flops 3072 | bytes 20480 | tf_op jit(solution)/shard_map/mul | solution.py:319
  2.9 0.1 fusion
  3.0 0.7 %maximum_maximum_fusion.rows_ref = bf16[32,128]{1,0:T(8,128)(2,1)} fusion(bf16[32,1]{1,0:T(8,128)(2,1)S(1)} %copy.12, bf16[32,64]{1,0:T(8,128)(2,1)S(1)} %fusion, bf16[128]{0:T(256)(128)(2,1)S(1)} %pad.2.clone), kind=kLoop, calls=%fused_computation.3 | loop fusion | flops 24576 | bytes 12608 | tf_op jit(solution)/shard_map/concatenate | solution.py:324
  3.6 54.5 %shard_map.95 = (f32[16,64]{1,0:T(8,128)}, f32[16,128]{1,0:T(8,128)}) custom-call(bf16[256,256]{1,0:T(8,128)(2,1)} %spectra_ref.1, bf16[256,2048]{1,0:T(8,128)(2,1)} %response_ref.1, bf16[32,128]{1,0:T(8,128)(2,1)} %maximum_maximum_fusion.rows_ref, f32[8,128]{1,0:T(8,128)} %bitcast.3), custom_call_target="tpu_custom_call" | custom-call | tf_op jit(solution)/shard_map/pallas_call | solution.py:339
  58.1 0.0 copy-start.1
  58.1 1.4 %reshape.15 = f32[1024]{0:T(1024)} reshape(f32[16,64]{1,0:T(8,128)} %get-tuple-element.4) | data formatting | bytes 8192 | tf_op jit(solution)/shard_map/reshape | solution.py:375
  59.5 0.0 copy-done.1
  59.5 0.1 reshape.16
  59.6 0.7 %copy.13 = f32[64,32]{0,1:T(8,128)} copy(f32[64,32]{1,0:T(8,128)S(1)} %reshape.16) | data formatting | bytes 16384
  (2 shorter events, 0.0 us)
Async XLA Ops:
  0.6 0.7 %copy-start.2 = (s32[32]{0:T(128)S(1)}, s32[32]{0:T(128)}, u32[]{:S(2)}) copy-start(s32[32]{0:T(128)} %param.13) | copy-start | bytes 388
  0.6 1.5 %copy-start = (f32[32,32]{1,0:T(8,128)S(1)}, f32[32,32]{1,0:T(8,128)}, u32[]{:S(2)}) copy-start(f32[32,32]{1,0:T(8,128)} %param.10) | copy-start | bytes 12292
  58.1 1.4 %copy-start.1 = (f32[16,128]{1,0:T(8,128)S(1)}, f32[16,128]{1,0:T(8,128)}, u32[]{:S(2)}) copy-start(f32[16,128]{1,0:T(8,128)} %get-tuple-element.5) | copy-start | bytes 24580

commit v2 on v1

--- a/solution.py
+++ b/solution.py
@@ -33,10 +33,15 @@
     galaxies,
     spectra_ref,
     response_ref,
-    rows_ref,
+    obs_ref,
+    ivar_ref,
+    mask_ref,
+    counts_ref,
+    anchors_ref,
     w_ref,
     outw_ref,
     outp_ref,
+    rows_f,
     part,
     got_a,
     got_b,
@@ -93,6 +98,19 @@
         part[k] = block.reshape(nz, 2, 2, models, width)
 
     flux_part(0)
+
+    own_g = obs_ref.shape[0]
+    eye = iota((own_g, own_g), 0) == iota((own_g, own_g), 1)
+
+    def column(row):
+        return jnp.sum(jnp.where(eye, row, 0.0), axis=1, keepdims=True)
+
+    masked_var = ivar_ref[...] * mask_ref[...].astype(jnp.float32)
+    temper = column(4.0 / (counts_ref[...].astype(jnp.float32) + 8.0))
+    rows_f[...] = jnp.broadcast_to(column(anchors_ref[...].astype(jnp.float32)), rows_f.shape)
+    rows_f[:, 0:BANDS] = temper * (masked_var * obs_ref[...])
+    rows_f[:, BANDS : 2 * BANDS] = temper * masked_var
+    all_rows[me] = rows_f[...].astype(jnp.bfloat16)
     pl.semaphore_wait(barrier, n - 1)
 
     def copy(src, dst, send, recv, target):
@@ -134,9 +152,8 @@
         return copy(src, dst, send.at[s], recv.at[s], lax.rem(me + s, n))
 
     def rows_copy(s):
-        return spread(rows_ref, all_rows.at[me], r_send, r_recv, s)
-
-    all_rows[me] = rows_ref[...]
+        return spread(all_rows.at[me], all_rows.at[me], r_send, r_recv, s)
+
 
     for k in range(CHUNKS):
         copy_a(k).wait()
@@ -179,7 +196,7 @@
         jnp.float32
     )
 
-    @pl.loop(0, n)
+    @pl.loop(0, n, unroll=4)
     def _(d):
         x = all_rows[d]
         x = jnp.concatenate([x] * QUARTERS, axis=0)
@@ -204,8 +221,18 @@
             cols[j * models : (j + 1) * models, LANES : 2 * LANES] = (-(f * f)).astype(jnp.bfloat16)
 
     rows_all = GROUPS_Z * models
-
-    @pl.loop(0, n)
+    quarter = iota((1, LANES), 1) // BANDS
+    norms[me] = jnp.zeros(norms.shape[1:], jnp.float32)
+    tots[me] = jnp.zeros(tots.shape[1:], jnp.float32)
+
+    def spread_out(slot, x):
+        for q in range(QUARTERS):
+            x_ref[slot, q] = over_quarters(jnp.where(quarter == q, x, 0.0), jnp.add)
+
+    def factor(slot, d):
+        return x_ref[slot, lax.rem(d, QUARTERS), pl.ds(d // QUARTERS, 1), :]
+
+    @pl.loop(0, n, unroll=4)
     def _(d):
         scores = lax.dot_general(
             cols[...], rt[d], (((1,), (1,)), ((), ())), preferred_element_type=jnp.float32
@@ -216,8 +243,10 @@
         e = jnp.exp(scores - peak)
         e_ref[d] = e
         total = over_quarters(jnp.sum(e * wts[...], axis=0, keepdims=True), jnp.add)
-        norms[me, 0, pl.ds(d, 1), :] = peak
-        norms[me, 1, pl.ds(d, 1), :] = total
+        mine = quarter == lax.rem(d, QUARTERS)
+        at = pl.ds(d // QUARTERS, 1)
+        norms[me, 0, at, :] = jnp.where(mine, peak, norms[me, 0, at, :])
+        norms[me, 1, at, :] = jnp.where(mine, total, norms[me, 1, at, :])
 
     def norms_copy(s):
         return spread(norms.at[me], norms.at[me], n_send, n_recv, s)
@@ -240,27 +269,30 @@
     total = jnp.zeros_like(top)
     for d in range(n):
         total = total + norms[d, 1] * jnp.exp(norms[d, 0] - top)
-    x_ref[0] = jnp.exp(norms[me, 0] - top)
-    x_ref[1] = x_ref[0] / total
+    shift = jnp.exp(norms[me, 0] - top)
+    spread_out(1, shift / total)
+    spread_out(0, shift)
 
     same = (iota((LANES, LANES), 0) // BANDS == iota((LANES, LANES), 1) // BANDS).astype(jnp.float32)
 
     def new_weights():
         def add(d, acc):
-            return acc + e_ref[d] * x_ref[1, pl.ds(d, 1), :]
-
-        mass = lax.fori_loop(0, n, add, jnp.zeros((rows_all, LANES), jnp.float32))
+            return acc + e_ref[d] * factor(1, d)
+
+        mass = lax.fori_loop(0, n, add, jnp.zeros((rows_all, LANES), jnp.float32), unroll=4)
         mass = jnp.dot(mass, same, precision=HIGHEST, preferred_element_type=jnp.float32)
         wts[...] = wts[...] * mass * (1.0 / galaxies)
 
     new_weights()
 
-    @pl.loop(0, n)
+    @pl.loop(0, n, unroll=4)
     def _(d):
         v = (e_ref[d] * wts[...]).reshape(GROUPS_Z, models, LANES)
-        u = jnp.sum(v, axis=1) * x_ref[0, pl.ds(d, 1), :]
+        u = jnp.sum(v, axis=1) * factor(0, d)
         post[d] = u
-        tots[me, pl.ds(d, 1), :] = over_quarters(jnp.sum(u, axis=0, keepdims=True), jnp.add)
+        total = over_quarters(jnp.sum(u, axis=0, keepdims=True), jnp.add)
+        at = pl.ds(d // QUARTERS, 1)
+        tots[me, at, :] = jnp.where(quarter == lax.rem(d, QUARTERS), total, tots[me, at, :])
 
     def tots_copy(s):
         return spread(tots.at[me], tots.at[me], t_send, t_recv, s)
@@ -288,7 +320,7 @@
     total = tots[0]
     for d in range(1, n):
         total = total + tots[d]
-    x_ref[1] = x_ref[0] / total
+    spread_out(1, shift / total)
     new_weights()
 
     out = jnp.zeros((models, REDSHIFTS), jnp.float32)
@@ -310,41 +342,31 @@
     for s in range(1, n):
         mine = mine + got_post[s]
     whole = over_quarters(jnp.sum(mine, axis=0, keepdims=True), jnp.add)
-    outp_ref[...] = mine / whole
-
-
-def galaxy_rows(observed, inv_var, band_mask, det_counts, anchor_bins):
-    masked_var = inv_var * band_mask.astype(jnp.float32)
-    temper = 4.0 / (det_counts.astype(jnp.float32) + 8.0)
-    joined = jnp.concatenate((masked_var * observed, masked_var), axis=1)
-    joined = temper[:, None] * joined
-    own = observed.shape[0]
-    last = jnp.zeros((own, LANES - 2 * BANDS - 1), jnp.float32)
-    anchors = anchor_bins.astype(jnp.float32)[:, None]
-    return jnp.concatenate((joined, anchors, last), axis=1).astype(jnp.bfloat16)
+    mine = mine / whole
+    for q in range(QUARTERS):
+        outp_ref[pl.ds(q, GROUPS_Z, stride=QUARTERS), :] = mine[:, q * BANDS : (q + 1) * BANDS]
 
 
 def on_device(
     n, spectra, response, observed, inv_var, band_mask, det_counts, anchor_bins, init_weights
 ):
-    rows = galaxy_rows(observed, inv_var, band_mask, det_counts, anchor_bins)
     own = observed.shape[0]
     models = spectra.shape[0] // n
     nz = n // 4
     width = response.shape[1] // CHUNKS
     f32, bf16 = jnp.float32, jnp.bfloat16
     dma = pltpu.SemaphoreType.DMA
-    lanes_g = QUARTERS * own
     rows_all = GROUPS_Z * models
     weights, posterior = pl.pallas_call(
         functools.partial(body, n, own * n),
         out_shape=(
             jax.ShapeDtypeStruct((models, REDSHIFTS), f32),
-            jax.ShapeDtypeStruct((GROUPS_Z, lanes_g), f32),
+            jax.ShapeDtypeStruct((REDSHIFTS, own), f32),
         ),
-        in_specs=[pl.BlockSpec(memory_space=pltpu.VMEM)] * 4,
+        in_specs=[pl.BlockSpec(memory_space=pltpu.VMEM)] * 8,
         out_specs=[pl.BlockSpec(memory_space=pltpu.VMEM)] * 2,
         scratch_shapes=[
+            pltpu.VMEM((own, LANES), f32),
             pltpu.VMEM((CHUNKS, nz, 2, 2, models, width), f32),
             pltpu.VMEM((CHUNKS, nz, 2, models, width), f32),
             pltpu.VMEM((CHUNKS, nz, models, width), f32),
@@ -355,9 +377,9 @@
             pltpu.VMEM((rows_all, 2 * LANES), bf16),
             pltpu.VMEM((n, rows_all, LANES), f32),
             pltpu.VMEM((rows_all, LANES), f32),
-            pltpu.VMEM((n, 2, n, LANES), f32),
-            pltpu.VMEM((2, n, LANES), f32),
-            pltpu.VMEM((n, n, LANES), f32),
+            pltpu.VMEM((n, 2, nz, LANES), f32),
+            pltpu.VMEM((2, QUARTERS, nz, LANES), f32),
+            pltpu.VMEM((n, nz, LANES), f32),
             pltpu.VMEM((n, GROUPS_Z, LANES), f32),
             pltpu.VMEM((n, GROUPS_Z, LANES), f32),
             dma((CHUNKS,)),
@@ -371,8 +393,17 @@
         compiler_params=pltpu.CompilerParams(
             collective_id=0, has_side_effects=True, vmem_limit_bytes=56 * 2**20
         ),
-    )(spectra, response, rows, init_weights.reshape(-1, LANES))
-    return weights.reshape(-1), posterior.reshape(REDSHIFTS, own)
+    )(
+        spectra,
+        response,
+        observed,
+        inv_var,
+        band_mask,
+        det_counts.reshape(1, own),
+        anchor_bins.reshape(1, own),
+        init_weights.reshape(-1, LANES),
+    )
+    return weights.reshape(-1), posterior
 
 
 def solution(mesh):

time: 60.6 us -> 47.3 us (0.78)
  Pallas kernels: 54.5 us -> 43.7 us
  other arithmetic: 2.17 us -> 0 us
    pallas_call x1, Pallas kernels: 54.5 us -> 43.7 us  [on_device(): pl.pallas_call(functools.partial(body, n, own * n), out_shape=(jax.ShapeD...]
    mul x1 -> x0, other arithmetic: 0.74 us -> none  [galaxy_rows(): joined = jnp.concatenate((masked_var * observed, masked_var), axis=1)]
    concatenate x1 -> x0, other arithmetic: 0.69 us -> none  [galaxy_rows(): return jnp.concatenate((joined, anchors, last), axis=1).astype(jnp.bfloat16)]
    broadcast_in_dim x1 -> x0, other arithmetic: 0.66 us -> none  [galaxy_rows(): anchors = anchor_bins.astype(jnp.float32)[:, None]]
    unnamed x7 -> x1, local copies, waits for them, and re-layouts: 1.33 us -> 1.44 us
    reshape x2 -> x1, local copies, waits for them, and re-layouts: 1.43 us -> 1.36 us  [on_device(): return (weights.reshape(-1), posterior)]
where the time goes in v2:
time: 47.3 us; the launch traced here: 47.1 us
  Pallas kernels  43.7 us (92%)
  local copies, waits for them, and re-layouts  2.79 us (6%)
  between operations  0.64 us (1%)
    pallas_call x1, Pallas kernels, on_device(): pl.pallas_call(functools.partial(body, n, own * n), out_shape=(jax.ShapeD...  43.7 us
    unnamed x1, local copies, waits for them, and re-layouts  1.44 us
    reshape x1, local copies, waits for them, and re-layouts, on_device(): return (weights.reshape(-1), posterior)  1.36 us

profile of v2, /device:TPU:0, one launch (start us, length us, event | category | flops | bytes accessed | tf_op | source)
XLA Modules:
  0.0 47.1 jit_solution(14358160137854666226)
XLA Ops:
  0.6 43.7 %shard_map.95 = (f32[16,64]{1,0:T(8,128)}, f32[64,32]{1,0:T(8,128)}) custom-call(bf16[256,256]{1,0:T(8,128)(2,1)} %spectra_ref.1, bf16[256,2048]{1,0:T(8,128)(2,1)} %response_ref.1, f32[32,32]{1,0:T(8,128)} %obs_ref.1, f32[32,32]{1,0:T(8,128)} %ivar_ref.1, s32[32,32]{1,0:T(8,128)} %mask_ref.1, s32[1,32]{1,0:T(1,128)} %bitcast.4, s32[1,32]{1,0:T(1,128)} %bitcast.5, ...), custom_call_target="tpu_custom_call" | custom-call | tf_op jit(solution)/shard_map/pallas_call | solution.py:360
  44.3 1.4 %reshape.19 = f32[1024]{0:T(1024)} reshape(f32[16,64]{1,0:T(8,128)} %get-tuple-element.4) | data formatting | bytes 8192 | tf_op jit(solution)/shard_map/reshape | solution.py:406
  45.7 1.4 %copy.10 = f32[64,32]{0,1:T(8,128)} copy(f32[64,32]{1,0:T(8,128)} %get-tuple-element.7) | data formatting | bytes 16384

commit v3 on v2

--- a/solution.py
+++ b/solution.py
@@ -196,7 +196,7 @@
         jnp.float32
     )
 
-    @pl.loop(0, n, unroll=4)
+    @pl.loop(0, n, unroll=8)
     def _(d):
         x = all_rows[d]
         x = jnp.concatenate([x] * QUARTERS, axis=0)
@@ -232,7 +232,7 @@
     def factor(slot, d):
         return x_ref[slot, lax.rem(d, QUARTERS), pl.ds(d // QUARTERS, 1), :]
 
-    @pl.loop(0, n, unroll=4)
+    @pl.loop(0, n, unroll=8)
     def _(d):
         scores = lax.dot_general(
             cols[...], rt[d], (((1,), (1,)), ((), ())), preferred_element_type=jnp.float32
@@ -279,13 +279,13 @@
         def add(d, acc):
             return acc + e_ref[d] * factor(1, d)
 
-        mass = lax.fori_loop(0, n, add, jnp.zeros((rows_all, LANES), jnp.float32), unroll=4)
+        mass = lax.fori_loop(0, n, add, jnp.zeros((rows_all, LANES), jnp.float32), unroll=8)
         mass = jnp.dot(mass, same, precision=HIGHEST, preferred_element_type=jnp.float32)
         wts[...] = wts[...] * mass * (1.0 / galaxies)
 
     new_weights()
 
-    @pl.loop(0, n, unroll=4)
+    @pl.loop(0, n, unroll=8)
     def _(d):
         v = (e_ref[d] * wts[...]).reshape(GROUPS_Z, models, LANES)
         u = jnp.sum(v, axis=1) * factor(0, d)
@@ -332,7 +332,11 @@
             precision=HIGHEST,
             preferred_element_type=jnp.float32,
         )
-    outw_ref[...] = out
+    rows_f[0:models, 0:REDSHIFTS] = out
+    for h in range(2):
+        outw_ref[:, h * REDSHIFTS : (h + 1) * REDSHIFTS] = rows_f[
+            pl.ds(h, models // 2, stride=2), 0:REDSHIFTS
+        ]
 
     @pl.loop(1, n)
     def _(s):
@@ -360,7 +364,7 @@
     weights, posterior = pl.pallas_call(
         functools.partial(body, n, own * n),
         out_shape=(
-            jax.ShapeDtypeStruct((models, REDSHIFTS), f32),
+            jax.ShapeDtypeStruct((models // 2, LANES), f32),
             jax.ShapeDtypeStruct((REDSHIFTS, own), f32),
         ),
         in_specs=[pl.BlockSpec(memory_space=pltpu.VMEM)] * 8,

time: 47.3 us -> 45.4 us (0.960)
  Pallas kernels: 43.7 us -> 42.6 us
  local copies, waits for them, and re-layouts: 2.79 us -> 2.04 us
    reshape x1 -> x0, local copies, waits for them, and re-layouts: 1.36 us -> none  [on_device(): return (weights.reshape(-1), posterior)]
    pallas_call x1, Pallas kernels: 43.7 us -> 42.6 us  [on_device(): pl.pallas_call(functools.partial(body, n, own * n), out_shape=(jax.ShapeD...]
    unnamed x1 -> x4, local copies, waits for them, and re-layouts: 1.44 us -> 2.04 us
where the time goes in v3:
time: 45.4 us; the launch traced here: 45.2 us
  Pallas kernels  42.6 us (94%)
  local copies, waits for them, and re-layouts  2.04 us (4%)
  between operations  0.65 us (1%)
    pallas_call x1, Pallas kernels, on_device(): pl.pallas_call(functools.partial(body, n, own * n), out_shape=(jax.ShapeD...  42.6 us
    unnamed x4, local copies, waits for them, and re-layouts  2.04 us

profile of v3, /device:TPU:0, one launch (start us, length us, event | category | flops | bytes accessed | tf_op | source)
XLA Modules:
  0.0 45.2 jit_solution(18171582132396205885)
XLA Ops:
  0.6 42.6 %shard_map.95 = (f32[8,128]{1,0:T(8,128)}, f32[64,32]{1,0:T(8,128)}) custom-call(bf16[256,256]{1,0:T(8,128)(2,1)} %spectra_ref.1, bf16[256,2048]{1,0:T(8,128)(2,1)} %response_ref.1, f32[32,32]{1,0:T(8,128)} %obs_ref.1, f32[32,32]{1,0:T(8,128)} %ivar_ref.1, s32[32,32]{1,0:T(8,128)} %mask_ref.1, s32[1,32]{1,0:T(1,128)} %bitcast.6, s32[1,32]{1,0:T(1,128)} %bitcast.7, ...), custom_call_target="tpu_custom_call" | custom-call | tf_op jit(solution)/shard_map/pallas_call | solution.py:364
  43.2 0.0 copy-start
  43.2 1.4 %copy.10 = f32[64,32]{0,1:T(8,128)} copy(f32[64,32]{1,0:T(8,128)} %get-tuple-element.7) | data formatting | bytes 16384
  44.6 0.0 copy-done
  44.6 0.6 %copy.12 = f32[1024]{0:T(1024)} copy(f32[1024]{0:T(1024)S(1)} %bitcast.5) | data formatting | bytes 8192
Async XLA Ops:
  43.2 1.5 %copy-start = (f32[8,128]{1,0:T(8,128)S(1)}, f32[8,128]{1,0:T(8,128)}, u32[]{:S(2)}) copy-start(f32[8,128]{1,0:T(8,128)} %get-tuple-element.4) | copy-start | bytes 12292
